TPU v7x, 32 devices: a whole 2x2x4 slice. The times are simulated.
32 devices in a mesh: gx: 8 (over z, y), gy: 2 (over x), col: 2 (over core).
Axes of the slice: x: 2, y: 2, z: 4, core: 2. Of those that a mesh axis runs over, the one named last changes fastest.
Arguments:
- particles: float32 [22, 8, 32, 12, 256], P(None, None, 'gx', 'gy', 'col'), may hold values from -1.6 to 1.6, as said below
- masses: float32 [8, 32, 12, 256], P(None, 'gx', 'gy', 'col'), may hold values from 0.06 to 0.19
- occupied: int32 [8, 32, 12, 256], P(None, 'gx', 'gy', 'col'), may hold values from 0 to 1, as said below
- node_flags: int32 [32, 12, 256], P('gx', 'gy', 'col'), may hold values from 0 to 2, as said below
- depart: int32 [8, 2, 2, 8, 128], P('gx', 'gy', 'col'), may hold values from 0 to 24575, as said below
- arrive: int32 [8, 2, 2, 8, 128], P('gx', 'gy', 'col'), may hold values from 0 to 3071, as said below
Outputs:
- final_state: float32 [9, 8, 32, 12, 256], P(None, None, 'gx', 'gy', 'col')
- arrivals: float32 [9, 8, 2, 2, 1024], P(None, 'gx', 'gy', 'col')
Inputs may be any that keep to these rules, and one draw needn't show every extreme that they name: `particles`: offsets lie in -0.5 .. 0.5; a particle listed in depart for direction (dx, dy) has its offset's x component between 0.4 and 0.5 times dx where dx is not 0, and likewise y; volumes lie in 0.08 .. 0.16. The scaffold fills some aligned 4 x 4 x 4 blocks of cells and leaves the others empty; in filled blocks most slots are occupied. `node_flags`: in every (x, y) column the lowest 1 to 3 nodes are 1 and the highest 1 to 3 nodes are 2; all others are 0. `depart`: all 1024 entries of a block are distinct; an entry for direction (dx, dy) names a slot of a cell with i = 3 where dx = 1, i = 0 where dx = -1, j = 5 where dy = 1, j = 0 where dy = -1. Some named slots are empty. arrive[b', d, e] is the cell (i * 6 + j) * 128 + k of block b' that lies across the block boundary from the cell of depart[b' - (dx, dy), d, e], moved by (dx, dy) with the same k.
All inputs are finite; a program needn't handle non-finite values.
Results may differ from a plain program's by a relative error of at most 0.0001.
Values sent between devices are 32-bit elements; how exact they have to be, the bound alone decides.
A program may use at most 128 MiB of HBM per device.

v0:
```python
import functools

import jax
import jax.numpy as jnp
from jax import lax
from jax.experimental import pallas as pl
from jax.experimental.pallas import tpu as pltpu
from jax.sharding import PartitionSpec as P

TIME_STEP = 0.2
LAME_FIRST = 2.5
SHEAR_MODULUS = 2.5
YIELD_STRESS = 1.2
MASS_FLOOR = 0.1
PLATEN_SPEED = 0.5
SHIFT_X = (-1, -1, -1, 0, 0, 1, 1, 1)
SHIFT_Y = (-1, 0, 1, -1, 1, -1, 0, 1)
STRESS_SLOT = ((0, 5, 4), (5, 1, 3), (4, 3, 2))
STRESS_PAIRS = ((0, 0), (1, 1), (2, 2), (1, 2), (0, 2), (0, 1))
F32 = jnp.float32


def spline(u):
    lo = 0.5 - u
    hi = 0.5 + u
    return (0.5 * lo * lo, 0.75 - u * u, 0.5 * hi * hi)


def advance(state, speed, moments):
    offset = state[0:3]
    grad = [[4.0 * (moments[b][k] - offset[b] * speed[k]) for b in range(3)] for k in range(3)]
    div = grad[0][0] + grad[1][1] + grad[2][2]
    trial = []
    for n in range(6):
        k, b = STRESS_PAIRS[n]
        if k == b:
            change = 2.0 * SHEAR_MODULUS * grad[k][k] + LAME_FIRST * div
        else:
            change = SHEAR_MODULUS * (grad[k][b] + grad[b][k])
        trial.append(state[15 + n] + TIME_STEP * change)
    pressure = (trial[0] + trial[1] + trial[2]) / 3.0
    dev = [trial[n] - pressure for n in range(3)] + trial[3:]
    square = (
        dev[0] * dev[0]
        + dev[1] * dev[1]
        + dev[2] * dev[2]
        + 2.0 * (dev[3] * dev[3] + dev[4] * dev[4] + dev[5] * dev[5])
    )
    factor = YIELD_STRESS / jnp.maximum(jnp.sqrt(1.5 * square), YIELD_STRESS)
    stress = [pressure + factor * dev[n] for n in range(3)] + [factor * dev[n] for n in range(3, 6)]
    return grad, div, stress


def kernel(
    S, X, Y, n_gx, n_gy,
    part, mass, occ, flags, rowq, kidx,
    out, arr,
    ST, PT, D, GZ, N0, N1, FL, VZ, VS, VALS, DM,
    PK, PKR, SYH0, SYL0, RYL0, RYH0, SYH1, SYL1, RYL1, RYH1,
    RXL0, RXH0, RXL1, RXH1, RES, ARR,
    send_sem, recv_sem,
):
    XE, YE = X + 4, Y + 4
    Z = 128
    R = S * X
    gx = lax.axis_index("gx")
    gy = lax.axis_index("gy")
    col = lax.axis_index("col")

    def at(dx, dy):
        return (lax.rem(gx + dx + n_gx, n_gx), lax.rem(gy + dy + n_gy, n_gy), col)

    sibling = (gx, gy, 1 - col)

    barrier = pltpu.get_barrier_semaphore()
    for dx, dy in zip(SHIFT_X, SHIFT_Y):
        pl.semaphore_signal(
            barrier, inc=1, device_id=at(dx, dy), device_id_type=pl.DeviceIdType.MESH
        )
    pl.semaphore_signal(barrier, inc=1, device_id=sibling, device_id_type=pl.DeviceIdType.MESH)

    def send(src, dst, slot, target):
        copy = pltpu.make_async_remote_copy(
            src_ref=src,
            dst_ref=dst,
            send_sem=send_sem.at[slot],
            recv_sem=recv_sem.at[slot],
            device_id=target,
            device_id_type=pl.DeviceIdType.MESH,
        )
        copy.start()
        return copy

    lane = lax.broadcasted_iota(jnp.int32, (YE, Z), 1)
    is_low = (lane * 0 + col) == 0
    row = lax.broadcasted_iota(jnp.int32, (Y, Z), 0)
    far_y = jnp.where(row == 0, -2.0, 2.0).astype(F32)

    def prepare(step):
        def body(q, carry):
            i = q // S
            s = q % S
            r = s * X + i
            if step == 0:
                st = [part[c, r] for c in range(22)]
            else:
                st = [ST[c, q] for c in range(22)]
            o = occ[r].astype(F32)
            m = mass[r] * o
            w = (4.0 * TIME_STEP) * (st[21] * o)
            ws = [w * st[15 + n] for n in range(6)]
            Q = [[m * st[6 + 3 * k + b] - ws[STRESS_SLOT[k][b]] for b in range(3)] for k in range(3)]
            anchor = [
                m * st[3 + k] - (Q[k][0] * st[0] + Q[k][1] * st[1] + Q[k][2] * st[2])
                for k in range(3)
            ]
            PT[0, q] = m
            for k in range(3):
                PT[1 + k, q] = anchor[k]
                for b in range(3):
                    PT[4 + 3 * k + b, q] = Q[k][b]
            if step == 0:
                for dim, base in ((0, 13), (1, 17)):
                    ws3 = spline(st[dim])
                    for e in range(3):
                        PT[base + e, q] = ws3[e]
            else:
                code = DM[q, 0:Y]
                zero = jnp.zeros_like(code)
                sx = jnp.where(code < 3.5, -1.0, jnp.where(code > 5.5, 1.0, 0.0))
                sx = jnp.where(code < 0.5, 0.0, sx)
                low_y = (code == 1.0) | (code == 4.0) | (code == 6.0)
                high_y = (code == 3.0) | (code == 5.0) | (code == 8.0)
                sy = jnp.where(low_y, -1.0, jnp.where(high_y, 1.0, 0.0))
                for dim, base, sh in ((0, 13, sx), (1, 17, sy)):
                    p0, p1, p2 = spline(st[dim] - sh)
                    up = sh > 0.5
                    down = sh < -0.5
                    PT[base, q] = jnp.where(up, zero, jnp.where(down, p1, p0))
                    PT[base + 1, q] = jnp.where(up, p0, jnp.where(down, p2, p1))
                    PT[base + 2, q] = jnp.where(up, p1, jnp.where(down, zero, p2))
                    PT[base + 3, q] = jnp.where(up, p2, jnp.where(down, p0, zero))
            wz = spline(st[2])
            for e in range(3):
                PT[21 + e, q] = wz[e]
            return carry

        lax.fori_loop(0, R, body, 0)

    def deposit(nb, pairs):
        D[...] = jnp.zeros(D.shape, F32)

        def body(p, carry):
            f = p // (3 * X)
            t = p - 3 * X
            i = (1 - f) * (p // 3) + f * (t * (X - 1))
            a = (1 - f) * (p % 3) + f * 3
            xi = (1 - f) * (p // 3 + 1 + p % 3) + f * (t * (X + 3))
            lever = ((1 - f) * (p % 3 - 1) + f * (4 * t - 2)).astype(F32)
            for b in range(nb):
                acc = [[None] * 4 for _ in range(3)]
                for s in range(S):
                    q = i * S + s
                    wxy = PT[13 + a, q] * PT[17 + b, q]
                    wz = [PT[21 + c, q] for c in range(3)]
                    mw = PT[0, q] * wxy
                    base = []
                    slope = []
                    for k in range(3):
                        v = PT[1 + k, q] + lever * PT[4 + 3 * k, q]
                        if b == 0:
                            v = v - PT[5 + 3 * k, q]
                        elif b == 2:
                            v = v + PT[5 + 3 * k, q]
                        elif b == 3:
                            v = v + far_y * PT[5 + 3 * k, q]
                        base.append(v * wxy)
                        slope.append(PT[6 + 3 * k, q] * wxy)
                    for c in range(3):
                        terms = [mw * wz[c]]
                        for k in range(3):
                            v = base[k]
                            if c == 0:
                                v = v - slope[k]
                            elif c == 2:
                                v = v + slope[k]
                            terms.append(v * wz[c])
                        for n in range(4):
                            acc[c][n] = terms[n] if acc[c][n] is None else acc[c][n] + terms[n]
                for c in range(3):
                    for n in range(4):
                        D[b, c, n, xi] = D[b, c, n, xi] + acc[c][n]
            return carry

        lax.fori_loop(0, pairs, body, 0)

    def combine(step, nb, N):
        def body(x, carry):
            for n in range(4):
                for c in range(3):
                    GZ[c, n, x] = jnp.zeros((YE, Z), F32)
                    for b in range(3):
                        GZ[c, n, x, 1 + b : 1 + b + Y] = (
                            GZ[c, n, x, 1 + b : 1 + b + Y] + D[b, c, n, x]
                        )
                    if nb == 4:
                        GZ[c, n, x, 0:1] = GZ[c, n, x, 0:1] + D[3, c, n, x, 0:1]
                        GZ[c, n, x, YE - 1 : YE] = (
                            GZ[c, n, x, YE - 1 : YE] + D[3, c, n, x, Y - 1 : Y]
                        )
            return carry

        lax.fori_loop(0, XE, body, 0)
        pack = jnp.zeros((YE, Z), F32)
        for n in range(4):
            for x in range(XE):
                g0 = GZ[0, n, x]
                g2 = pltpu.roll(GZ[2, n, x], 1, 1)
                N[n, x] = (
                    GZ[1, n, x]
                    + jnp.where(lane < Z - 1, pltpu.roll(g0, Z - 1, 1), 0.0)
                    + jnp.where(lane > 0, g2, 0.0)
                )
                edge = jnp.where(is_low, g2, g0)
                l = n * XE + x
                moved = edge if l == 0 else pltpu.roll(edge, l, 1)
                pack = jnp.where(lane == l, moved, pack)
        PK[2 * step] = pack

    def unpack(value, l):
        return value if l == 0 else pltpu.roll(value, Z - l, 1)

    def velocities(step, N, SYH, SYL, RYL, RYH, RXL, RXH):
        nc = N.shape[0]
        nb = 3 if step == 0 else 4
        base = 6 * step
        if step == 0:
            N[4] = jnp.zeros((XE, YE, Z), F32)
            for x in range(X):
                N[4, x + 2, 2 : 2 + Y] = flags[x].astype(F32)
            pl.semaphore_wait(barrier, 9)
        copy = send(PK.at[2 * step], PKR.at[2 * step], base, sibling)
        copy.wait()
        got = PKR[2 * step]
        got = jnp.where(is_low, pltpu.roll(got, Z - 1, 1), got)
        at_edge = lane == jnp.where(is_low, Z - 1, 0)
        for n in range(4):
            for x in range(XE):
                N[n, x] = N[n, x] + jnp.where(at_edge, unpack(got, n * XE + x), 0.0)
        for n in range(nc):
            for x in range(XE):
                SYH[n, x] = N[n, x, Y : Y + 4]
                SYL[n, x] = N[n, x, 0:4]
        up = send(SYH, RYL, base + 1, at(0, 1))
        down = send(SYL, RYH, base + 2, at(0, -1))
        up.wait()
        down.wait()
        for n in range(nc):
            for x in range(XE):
                N[n, x, 0:4] = N[n, x, 0:4] + RYL[n, x]
                N[n, x, Y : Y + 4] = N[n, x, Y : Y + 4] + RYH[n, x]
        up = send(N.at[:, X : X + 4], RXL, base + 3, at(1, 0))
        down = send(N.at[:, 0:4], RXH, base + 4, at(-1, 0))
        up.wait()
        down.wait()
        pack = jnp.zeros((YE, Z), F32)
        for x in range(XE):
            tot = []
            for n in range(nc):
                v = N[n, x]
                if x < 4:
                    v = v + RXL[n, x]
                if x >= X:
                    v = v + RXH[n, x - X]
                tot.append(v)
            if step == 0:
                FL[x] = tot[4]
                fl = tot[4]
            else:
                fl = FL[x]
            inv = 1.0 / jnp.maximum(tot[0], MASS_FLOOR)
            for k in range(3):
                v = jnp.where(fl == 1.0, 0.0, tot[1 + k] * inv)
                if k == 2:
                    v = jnp.where(fl == 2.0, -PLATEN_SPEED, v)
                VZ[1, k, x] = v
                edge = jnp.where(is_low, pltpu.roll(v, 1, 1), v)
                l = k * XE + x
                moved = edge if l == 0 else pltpu.roll(edge, l, 1)
                pack = jnp.where(lane == l, moved, pack)
        PK[2 * step + 1] = pack
        copy = send(PK.at[2 * step + 1], PKR.at[2 * step + 1], base + 5, sibling)
        copy.wait()
        got = PKR[2 * step + 1]
        got = jnp.where(is_low, pltpu.roll(got, Z - 1, 1), got)
        got_high = jnp.where(is_low, got, 0.0)
        got_low = jnp.where(is_low, 0.0, got)
        if step == 0:
            VS[...] = jnp.zeros(VS.shape, F32)
        for k in range(3):
            for x in range(XE):
                l = k * XE + x
                v = VZ[1, k, x]
                VZ[0, k, x] = jnp.where(lane == 0, unpack(got_low, l), pltpu.roll(v, 1, 1))
                VZ[2, k, x] = jnp.where(
                    lane == Z - 1, unpack(got_high, l), pltpu.roll(v, Z - 1, 1)
                )

        def body(x, carry):
            for c in range(3):
                for k in range(3):
                    for b in range(3):
                        VS[b, c, k, x] = VZ[c, k, x, 1 + b : 1 + b + Y]
                    if nb == 4:
                        VS[3, c, k, x, 0:1] = VZ[c, k, x, 0:1]
                        VS[3, c, k, x, Y - 1 : Y] = VZ[c, k, x, YE - 1 : YE]
            return carry

        lax.fori_loop(0, XE, body, 0)

    def gather(step):
        nab = 3 if step == 0 else 4

        def body(q, carry):
            i = q // S
            s = q % S
            r = s * X + i
            side = i // (X - 1)
            wz = [PT[21 + c, q] for c in range(3)]
            wy = [PT[17 + b, q] for b in range(nab)]
            speed = [None] * 3
            mx = [None] * 3
            my = [None] * 3
            mz = [None] * 3

            def plus(total, term):
                return term if total is None else total + term

            for a in range(nab):
                xi = i + 1 + a if a < 3 else side * (X + 3)
                u = [None] * 3
                uy = [None] * 3
                uz = [None] * 3
                for b in range(nab):
                    for k in range(3):
                        low = wz[0] * VS[b, 0, k, xi]
                        mid = wz[1] * VS[b, 1, k, xi]
                        high = wz[2] * VS[b, 2, k, xi]
                        t = wy[b] * (low + mid + high)
                        u[k] = plus(u[k], t)
                        if b == 0:
                            uy[k] = -t
                        elif b == 2:
                            uy[k] = uy[k] + t
                        elif b == 3:
                            uy[k] = uy[k] + far_y * t
                        uz[k] = plus(uz[k], wy[b] * (high - low))
                wx = PT[13 + a, q]
                for k in range(3):
                    t = wx * u[k]
                    speed[k] = plus(speed[k], t)
                    if a == 0:
                        mx[k] = -t
                    elif a == 2:
                        mx[k] = mx[k] + t
                    elif a == 3:
                        mx[k] = mx[k] + (4 * side - 2).astype(F32) * t
                    my[k] = plus(my[k], wx * uy[k])
                    mz[k] = plus(mz[k], wx * uz[k])
            moments = [mx, my, mz]
            src = part if step == 0 else ST
            idx = r if step == 0 else q
            state = [src[c, idx] for c in range(22)]
            grad, div, stress = advance(state, speed, moments)
            if step == 0:
                for k in range(3):
                    ST[k, q] = state[k] + TIME_STEP * speed[k]
                    ST[3 + k, q] = speed[k]
                    for b in range(3):
                        ST[6 + 3 * k + b, q] = grad[k][b]
                for n in range(6):
                    ST[15 + n, q] = stress[n]
                ST[21, q] = state[21] * (1.0 + TIME_STEP * div)
            else:
                o = occ[r].astype(F32)
                stay = jnp.where(DM[q, 0:Y] < 0.5, o, 0.0)
                for n, v in enumerate(speed + stress):
                    out[n, r] = v * stay
                    VALS[n, q, 0:Y] = v * o
            return carry

        lax.fori_loop(0, R, body, 0)

    def direction_map():
        rows = lax.broadcasted_iota(jnp.int32, (R * 8, Z), 0)
        ks = lax.broadcasted_iota(jnp.int32, (Z, Z), 0)
        total = jnp.zeros((R * 8, Z), F32)
        for d in range(8):
            here = jnp.where(rows == rowq[d : d + 1, :], d + 1.0, 0.0).astype(jnp.bfloat16)
            hot = jnp.where(ks == kidx[d : d + 1, :], 1.0, 0.0).astype(jnp.bfloat16)
            total = total + lax.dot_general(
                here, hot, (((1,), (1,)), ((), ())), preferred_element_type=F32
            )
        DM[...] = total.reshape(R, 8, Z)

    def extract():
        ks = lax.broadcasted_iota(jnp.int32, (Z, Z), 0)
        copies = []
        for d in range(8):
            first, count = {-1: (0, S), 0: (0, R), 1: (R - S, S)}[SHIFT_X[d]]
            rows = lax.broadcasted_iota(jnp.int32, (count * 8, Z), 0) + first * 8
            here = rows == rowq[d : d + 1, :]
            hot = jnp.where(ks == kidx[d : d + 1, :], 1.0, 0.0).astype(jnp.bfloat16)
            for n in range(9):
                v = VALS[n, first : first + count].reshape(count * 8, Z)
                hi = v.astype(jnp.bfloat16)
                lo = (v - hi.astype(F32)).astype(jnp.bfloat16)
                t = jnp.dot(hi, hot, preferred_element_type=F32) + jnp.dot(
                    lo, hot, preferred_element_type=F32
                )
                RES[d, n : n + 1] = jnp.sum(jnp.where(here, t, 0.0), axis=0, keepdims=True)
            copies.append(
                send(RES.at[d], ARR.at[d], 12 + d, at(SHIFT_X[d], SHIFT_Y[d]))
            )
        for copy in copies:
            copy.wait()
        for d in range(8):
            arr[:, d] = ARR[d]

    prepare(0)
    deposit(3, 3 * X)
    combine(0, 3, N0)
    velocities(0, N0, SYH0, SYL0, RYL0, RYH0, RXL0, RXH0)
    direction_map()
    VALS[...] = jnp.zeros(VALS.shape, F32)
    gather(0)
    prepare(1)
    deposit(4, 3 * X + 2)
    combine(1, 4, N1)
    velocities(1, N1, SYH1, SYL1, RYL1, RYH1, RXL1, RXH1)
    gather(1)
    extract()


def body(n_gx, n_gy, particles, masses, occupied, node_flags, depart, arrive):
    _, S, X, Y, Z = particles.shape
    R, XE, YE = S * X, X + 4, Y + 4
    leaving = depart.reshape(8, Z)
    slot = leaving // (X * Y * Z)
    i = leaving // (Y * Z) % X
    j = leaving // Z % Y
    rowq = (i * S + slot) * 8 + j
    kidx = leaving % Z
    vmem = lambda *shape: pltpu.VMEM(shape, F32)
    final_state, arrivals = pl.pallas_call(
        functools.partial(kernel, S, X, Y, n_gx, n_gy),
        out_shape=(
            jax.ShapeDtypeStruct((9, R, Y, Z), F32),
            jax.ShapeDtypeStruct((9, 8, Z), F32),
        ),
        in_specs=[pl.BlockSpec(memory_space=pltpu.VMEM)] * 6,
        out_specs=(pl.BlockSpec(memory_space=pltpu.VMEM),) * 2,
        scratch_shapes=[
            vmem(22, R, Y, Z),
            vmem(24, R, Y, Z),
            vmem(4, 3, 4, XE, Y, Z),
            vmem(3, 4, XE, YE, Z),
            vmem(5, XE, YE, Z),
            vmem(4, XE, YE, Z),
            vmem(XE, YE, Z),
            vmem(3, 3, XE, YE, Z),
            vmem(4, 3, 3, XE, Y, Z),
            vmem(9, R, 8, Z),
            vmem(R, 8, Z),
            vmem(4, YE, Z),
            vmem(4, YE, Z),
            vmem(5, XE, 4, Z),
            vmem(5, XE, 4, Z),
            vmem(5, XE, 4, Z),
            vmem(5, XE, 4, Z),
            vmem(4, XE, 4, Z),
            vmem(4, XE, 4, Z),
            vmem(4, XE, 4, Z),
            vmem(4, XE, 4, Z),
            vmem(5, 4, YE, Z),
            vmem(5, 4, YE, Z),
            vmem(4, 4, YE, Z),
            vmem(4, 4, YE, Z),
            vmem(8, 9, Z),
            vmem(8, 9, Z),
            pltpu.SemaphoreType.DMA((20,)),
            pltpu.SemaphoreType.DMA((20,)),
        ],
        compiler_params=pltpu.CompilerParams(
            collective_id=0, has_side_effects=True, vmem_limit_bytes=60 * 1024 * 1024
        ),
        name="steps",
    )(
        particles.reshape(22, R, Y, Z),
        masses.reshape(R, Y, Z),
        occupied.reshape(R, Y, Z),
        node_flags,
        rowq,
        kidx,
    )
    return final_state.reshape(9, S, X, Y, Z), arrivals.reshape(9, 1, 1, 1, 8 * Z)


def solution(mesh):
    in_specs = (
        P(None, None, "gx", "gy", "col"),
        P(None, "gx", "gy", "col"),
        P(None, "gx", "gy", "col"),
        P("gx", "gy", "col"),
        P("gx", "gy", "col", None, None),
        P("gx", "gy", "col", None, None),
    )
    out_specs = (P(None, None, "gx", "gy", "col"), P(None, "gx", "gy", "col", None))
    sizes = mesh.shape
    assert sizes["col"] == 2
    return jax.shard_map(
        functools.partial(body, sizes["gx"], sizes["gy"]),
        mesh=mesh,
        in_specs=in_specs,
        out_specs=out_specs,
        check_vma=False,
    )
```

profile of v0, /device:TPU:0, one launch (start us, length us, event | category | flops | bytes accessed | tf_op | source)
XLA Modules:
  0.0 72.8 jit_solution(12638098974315357393)
XLA Ops:
  0.6 1.3 %add_select_fusion = (s32[8,128]{1,0:T(8,128)}, s32[8,128]{1,0:T(8,128)}) fusion(s32[1,1,1,8,128]{4,3,2,1,0:T(8,128)} %param.10), kind=kLoop, calls=%fused_computation | loop fusion | flops 53248 | bytes 12288 | tf_op jit(solution)/shard_map/jit(remainder)/select_n | solution.py:453
  1.9 1.3 %copy.16.flags = s32[4,6,128]{2,1,0:T(8,128)} copy(s32[4,6,128]{2,0,1:T(4,128)} %param.9) | data formatting | bytes 24576 | tf_op args[3]
  3.2 1.6 %copy.14 = f32[8,4,6,128]{3,2,1,0:T(8,128)} copy(f32[8,4,6,128]{3,1,2,0:T(4,128)} %param.7) | data formatting | bytes 196608 | tf_op args[1]
  4.8 1.5 %copy.15 = s32[8,4,6,128]{3,2,1,0:T(8,128)} copy(s32[8,4,6,128]{3,1,2,0:T(4,128)} %param.8) | data formatting | bytes 196608 | tf_op args[2]
  6.4 3.7 %copy.13 = f32[22,8,4,6,128]{4,3,2,1,0:T(8,128)} copy(f32[22,8,4,6,128]{4,2,3,1,0:T(4,128)} %param.6) | data formatting | bytes 4325376 | tf_op args[0]
  10.1 58.9 %steps.1 = (f32[9,32,6,128]{3,2,1,0:T(8,128)}, f32[9,8,128]{2,1,0:T(8,128)}) custom-call(f32[22,32,6,128]{3,2,1,0:T(8,128)} %bitcast.53, f32[32,6,128]{2,1,0:T(8,128)} %bitcast.55, s32[32,6,128]{2,1,0:T(8,128)} %bitcast.56, s32[4,6,128]{2,1,0:T(8,128)} %copy.16.flags, s32[8,128]{1,0:T(8,128)} %get-tuple-element.11.rowq, s32[8,128]{1,0:T(8,128)} %get-tuple-element.10.kidx), custom_call_target="tpu_custom_call" | custom-call | tf_op jit(solution)/shard_map/steps/pallas_call | solution.py:455
  69.0 2.4 %copy.17 = f32[9,8,4,6,128]{4,2,3,1,0:T(4,128)} copy(f32[9,8,4,6,128]{4,3,2,1,0:T(8,128)} %bitcast.54) | data formatting | bytes 1769472
  71.4 1.4 %copy.20 = f32[9,1,1,1,1024]{4,3,2,1,0:T(1,128)} copy(f32[9,1,1,1,1024]{4,3,2,1,0:T(1,128)} %bitcast.57) | data formatting | bytes 73728
where the time goes:
time: 73.2 us; the launch traced here: 72.8 us
  Pallas kernels  58.9 us (80%)
  local copies, waits for them, and re-layouts  11.9 us (16%)
  other arithmetic  1.3 us (2%)
    pallas_call x1, Pallas kernels, body(): pl.pallas_call(functools.partial(kernel, S, X, Y, n_gx, n_gy), out_shape=...  58.9 us
    unnamed x6, local copies, waits for them, and re-layouts  11.9 us

commit v1 on v0

--- a/solution.py
+++ b/solution.py
@@ -53,11 +53,11 @@
 
 def kernel(
     S, X, Y, n_gx, n_gy,
-    part, mass, occ, flags, rowq, kidx,
+    part, mass, occ, flags, depart,
     out, arr,
     ST, PT, D, GZ, N0, N1, FL, VZ, VS, VALS, DM,
     PK, PKR, SYH0, SYL0, RYL0, RYH0, SYH1, SYL1, RYL1, RYH1,
-    RXL0, RXH0, RXL1, RXH1, RES, ARR,
+    RXL0, RXH0, RXL1, RXH1, NF, SFH, SFL, RFYL, RFYH, RFXL, RFXH, RES, ARR,
     send_sem, recv_sem,
 ):
     XE, YE = X + 4, Y + 4
@@ -100,13 +100,12 @@
         def body(q, carry):
             i = q // S
             s = q % S
-            r = s * X + i
             if step == 0:
-                st = [part[c, r] for c in range(22)]
+                st = [part[c, s, pl.ds(i, Y, stride=X), :] for c in range(22)]
             else:
                 st = [ST[c, q] for c in range(22)]
-            o = occ[r].astype(F32)
-            m = mass[r] * o
+            o = occ[s, pl.ds(i, Y, stride=X), :].astype(F32)
+            m = mass[s, pl.ds(i, Y, stride=X), :] * o
             w = (4.0 * TIME_STEP) * (st[21] * o)
             ws = [w * st[15 + n] for n in range(6)]
             Q = [[m * st[6 + 3 * k + b] - ws[STRESS_SLOT[k][b]] for b in range(3)] for k in range(3)]
@@ -210,10 +209,11 @@
                         )
             return carry
 
-        lax.fori_loop(0, XE, body, 0)
+        h = 1 + step
+        lax.fori_loop(2 - h, X + 2 + h, body, 0)
         pack = jnp.zeros((YE, Z), F32)
         for n in range(4):
-            for x in range(XE):
+            for x in range(2 - h, X + 2 + h):
                 g0 = GZ[0, n, x]
                 g2 = pltpu.roll(GZ[2, n, x], 1, 1)
                 N[n, x] = (
@@ -231,53 +231,78 @@
         return value if l == 0 else pltpu.roll(value, Z - l, 1)
 
     def velocities(step, N, SYH, SYL, RYL, RYH, RXL, RXH):
-        nc = N.shape[0]
+        h = 1 + step
+        lo = 2 - h
+        xs = range(lo, X + 2 + h)
         nb = 3 if step == 0 else 4
         base = 6 * step
+        flag_copies = []
         if step == 0:
-            N[4] = jnp.zeros((XE, YE, Z), F32)
+            NF[...] = jnp.zeros(NF.shape, F32)
             for x in range(X):
-                N[4, x + 2, 2 : 2 + Y] = flags[x].astype(F32)
+                fl = flags[pl.ds(x, Y, stride=X), :].astype(F32)
+                NF[x + 2, 2 : 2 + Y] = fl
+                SFH[x] = jnp.concatenate([fl[Y - 2 : Y], jnp.zeros((2, Z), F32)], axis=0)
+                SFL[x] = jnp.concatenate([jnp.zeros((2, Z), F32), fl[0:2]], axis=0)
             pl.semaphore_wait(barrier, 9)
+            flag_copies = [send(SFH, RFYL, 20, at(0, 1)), send(SFL, RFYH, 21, at(0, -1))]
         copy = send(PK.at[2 * step], PKR.at[2 * step], base, sibling)
         copy.wait()
         got = PKR[2 * step]
         got = jnp.where(is_low, pltpu.roll(got, Z - 1, 1), got)
         at_edge = lane == jnp.where(is_low, Z - 1, 0)
         for n in range(4):
-            for x in range(XE):
-                N[n, x] = N[n, x] + jnp.where(at_edge, unpack(got, n * XE + x), 0.0)
-        for n in range(nc):
-            for x in range(XE):
-                SYH[n, x] = N[n, x, Y : Y + 4]
-                SYL[n, x] = N[n, x, 0:4]
+            for x in xs:
+                v = N[n, x] + jnp.where(at_edge, unpack(got, n * XE + x), 0.0)
+                N[n, x] = v
+                SYH[n, x - lo] = v[Y + lo : Y + lo + 2 * h]
+                SYL[n, x - lo] = v[lo : lo + 2 * h]
         up = send(SYH, RYL, base + 1, at(0, 1))
         down = send(SYL, RYH, base + 2, at(0, -1))
+        for copy in flag_copies:
+            copy.wait()
+        flag_copies = []
+        if step == 0:
+            for x in range(X):
+                NF[x + 2, 0:4] = NF[x + 2, 0:4] + RFYL[x]
+                NF[x + 2, Y : Y + 4] = NF[x + 2, Y : Y + 4] + RFYH[x]
+            flag_copies = [
+                send(NF.at[X : X + 4], RFXL, 22, at(1, 0)),
+                send(NF.at[0:4], RFXH, 23, at(-1, 0)),
+            ]
         up.wait()
         down.wait()
-        for n in range(nc):
+        for n in range(4):
+            for x in xs:
+                N[n, x, lo : lo + 2 * h] = N[n, x, lo : lo + 2 * h] + RYL[n, x - lo]
+                N[n, x, Y + lo : Y + lo + 2 * h] = (
+                    N[n, x, Y + lo : Y + lo + 2 * h] + RYH[n, x - lo]
+                )
+        up = send(N.at[:, X + lo : X + lo + 2 * h], RXL, base + 3, at(1, 0))
+        down = send(N.at[:, lo : lo + 2 * h], RXH, base + 4, at(-1, 0))
+        for copy in flag_copies:
+            copy.wait()
+        if step == 0:
             for x in range(XE):
-                N[n, x, 0:4] = N[n, x, 0:4] + RYL[n, x]
-                N[n, x, Y : Y + 4] = N[n, x, Y : Y + 4] + RYH[n, x]
-        up = send(N.at[:, X : X + 4], RXL, base + 3, at(1, 0))
-        down = send(N.at[:, 0:4], RXH, base + 4, at(-1, 0))
+                v = NF[x]
+                if x < 4:
+                    v = v + RFXL[x]
+                if x >= X:
+                    v = v + RFXH[x - X]
+                FL[x] = v
         up.wait()
         down.wait()
         pack = jnp.zeros((YE, Z), F32)
-        for x in range(XE):
+        for x in xs:
             tot = []
-            for n in range(nc):
+            for n in range(4):
                 v = N[n, x]
-                if x < 4:
-                    v = v + RXL[n, x]
-                if x >= X:
-                    v = v + RXH[n, x - X]
+                if x < lo + 2 * h:
+                    v = v + RXL[n, x - lo]
+                if x >= X + lo:
+                    v = v + RXH[n, x - X - lo]
                 tot.append(v)
-            if step == 0:
-                FL[x] = tot[4]
-                fl = tot[4]
-            else:
-                fl = FL[x]
+            fl = FL[x]
             inv = 1.0 / jnp.maximum(tot[0], MASS_FLOOR)
             for k in range(3):
                 v = jnp.where(fl == 1.0, 0.0, tot[1 + k] * inv)
@@ -298,7 +323,7 @@
         if step == 0:
             VS[...] = jnp.zeros(VS.shape, F32)
         for k in range(3):
-            for x in range(XE):
+            for x in xs:
                 l = k * XE + x
                 v = VZ[1, k, x]
                 VZ[0, k, x] = jnp.where(lane == 0, unpack(got_low, l), pltpu.roll(v, 1, 1))
@@ -316,15 +341,14 @@
                         VS[3, c, k, x, Y - 1 : Y] = VZ[c, k, x, YE - 1 : YE]
             return carry
 
-        lax.fori_loop(0, XE, body, 0)
+        lax.fori_loop(lo, X + 2 + h, body, 0)
 
     def gather(step):
         nab = 3 if step == 0 else 4
 
-        def body(q, carry):
+        def body(na, q, carry):
             i = q // S
             s = q % S
-            r = s * X + i
             side = i // (X - 1)
             wz = [PT[21 + c, q] for c in range(3)]
             wy = [PT[17 + b, q] for b in range(nab)]
@@ -336,7 +360,7 @@
             def plus(total, term):
                 return term if total is None else total + term
 
-            for a in range(nab):
+            for a in range(na):
                 xi = i + 1 + a if a < 3 else side * (X + 3)
                 u = [None] * 3
                 uy = [None] * 3
@@ -368,9 +392,10 @@
                     my[k] = plus(my[k], wx * uy[k])
                     mz[k] = plus(mz[k], wx * uz[k])
             moments = [mx, my, mz]
-            src = part if step == 0 else ST
-            idx = r if step == 0 else q
-            state = [src[c, idx] for c in range(22)]
+            if step == 0:
+                state = [part[c, s, pl.ds(i, Y, stride=X), :] for c in range(22)]
+            else:
+                state = [ST[c, q] for c in range(22)]
             grad, div, stress = advance(state, speed, moments)
             if step == 0:
                 for k in range(3):
@@ -382,18 +407,31 @@
                     ST[15 + n, q] = stress[n]
                 ST[21, q] = state[21] * (1.0 + TIME_STEP * div)
             else:
-                o = occ[r].astype(F32)
+                o = occ[s, pl.ds(i, Y, stride=X), :].astype(F32)
                 stay = jnp.where(DM[q, 0:Y] < 0.5, o, 0.0)
                 for n, v in enumerate(speed + stress):
-                    out[n, r] = v * stay
+                    out[n, s, pl.ds(i, Y, stride=X), :] = v * stay
                     VALS[n, q, 0:Y] = v * o
             return carry
 
-        lax.fori_loop(0, R, body, 0)
+        if step == 0:
+            lax.fori_loop(0, R, functools.partial(body, 3), 0)
+        else:
+            edge_body = lambda t, carry: body(4, t + (t // S) * (R - 2 * S), carry)
+            lax.fori_loop(0, 2 * S, edge_body, 0)
+            lax.fori_loop(S, R - S, functools.partial(body, 3), 0)
+
+    ident = depart[...].astype(F32)
+    line = jnp.floor((ident + 0.5) * (1.0 / Z))
+    kidx = ident - line * Z
+    slot = jnp.floor((line + 0.5) * (1.0 / (X * Y)))
+    cell = line - slot * (X * Y)
+    cell_x = jnp.floor((cell + 0.5) * (1.0 / Y))
+    rowq = (cell_x * S + slot) * 8.0 + (cell - cell_x * Y)
 
     def direction_map():
-        rows = lax.broadcasted_iota(jnp.int32, (R * 8, Z), 0)
-        ks = lax.broadcasted_iota(jnp.int32, (Z, Z), 0)
+        rows = lax.broadcasted_iota(jnp.int32, (R * 8, Z), 0).astype(F32)
+        ks = lax.broadcasted_iota(jnp.int32, (Z, Z), 0).astype(F32)
         total = jnp.zeros((R * 8, Z), F32)
         for d in range(8):
             here = jnp.where(rows == rowq[d : d + 1, :], d + 1.0, 0.0).astype(jnp.bfloat16)
@@ -404,24 +442,30 @@
         DM[...] = total.reshape(R, 8, Z)
 
     def extract():
-        ks = lax.broadcasted_iota(jnp.int32, (Z, Z), 0)
+        ks = lax.broadcasted_iota(jnp.int32, (Z, Z), 0).astype(F32)
         copies = []
-        for d in range(8):
-            first, count = {-1: (0, S), 0: (0, R), 1: (R - S, S)}[SHIFT_X[d]]
-            rows = lax.broadcasted_iota(jnp.int32, (count * 8, Z), 0) + first * 8
-            here = rows == rowq[d : d + 1, :]
-            hot = jnp.where(ks == kidx[d : d + 1, :], 1.0, 0.0).astype(jnp.bfloat16)
+        for first, count, ds in ((0, S, (0, 1, 2)), (R - S, S, (5, 6, 7)), (0, R, (3, 4))):
+            rows = lax.broadcasted_iota(jnp.int32, (count * 8, Z), 0).astype(F32) + first * 8.0
+            hot = jnp.concatenate(
+                [jnp.where(ks == kidx[d : d + 1, :], 1.0, 0.0) for d in ds], axis=1
+            ).astype(jnp.bfloat16)
+            hot = jnp.concatenate([hot, hot], axis=0)
             for n in range(9):
                 v = VALS[n, first : first + count].reshape(count * 8, Z)
                 hi = v.astype(jnp.bfloat16)
-                lo = (v - hi.astype(F32)).astype(jnp.bfloat16)
-                t = jnp.dot(hi, hot, preferred_element_type=F32) + jnp.dot(
-                    lo, hot, preferred_element_type=F32
+                low = (v - hi.astype(F32)).astype(jnp.bfloat16)
+                t = jnp.dot(
+                    jnp.concatenate([hi, low], axis=1), hot, preferred_element_type=F32
                 )
-                RES[d, n : n + 1] = jnp.sum(jnp.where(here, t, 0.0), axis=0, keepdims=True)
-            copies.append(
-                send(RES.at[d], ARR.at[d], 12 + d, at(SHIFT_X[d], SHIFT_Y[d]))
-            )
+                for e, d in enumerate(ds):
+                    here = rows == rowq[d : d + 1, :]
+                    RES[d, n : n + 1] = jnp.sum(
+                        jnp.where(here, t[:, e * Z : (e + 1) * Z], 0.0), axis=0, keepdims=True
+                    )
+            for d in ds:
+                copies.append(
+                    send(RES.at[d], ARR.at[d], 12 + d, at(SHIFT_X[d], SHIFT_Y[d]))
+                )
         for copy in copies:
             copy.wait()
         for d in range(8):
@@ -445,27 +489,21 @@
 def body(n_gx, n_gy, particles, masses, occupied, node_flags, depart, arrive):
     _, S, X, Y, Z = particles.shape
     R, XE, YE = S * X, X + 4, Y + 4
-    leaving = depart.reshape(8, Z)
-    slot = leaving // (X * Y * Z)
-    i = leaving // (Y * Z) % X
-    j = leaving // Z % Y
-    rowq = (i * S + slot) * 8 + j
-    kidx = leaving % Z
     vmem = lambda *shape: pltpu.VMEM(shape, F32)
     final_state, arrivals = pl.pallas_call(
         functools.partial(kernel, S, X, Y, n_gx, n_gy),
         out_shape=(
-            jax.ShapeDtypeStruct((9, R, Y, Z), F32),
+            jax.ShapeDtypeStruct((9, S, Y * X, Z), F32),
             jax.ShapeDtypeStruct((9, 8, Z), F32),
         ),
-        in_specs=[pl.BlockSpec(memory_space=pltpu.VMEM)] * 6,
+        in_specs=[pl.BlockSpec(memory_space=pltpu.VMEM)] * 5,
         out_specs=(pl.BlockSpec(memory_space=pltpu.VMEM),) * 2,
         scratch_shapes=[
             vmem(22, R, Y, Z),
             vmem(24, R, Y, Z),
             vmem(4, 3, 4, XE, Y, Z),
             vmem(3, 4, XE, YE, Z),
-            vmem(5, XE, YE, Z),
+            vmem(4, XE, YE, Z),
             vmem(4, XE, YE, Z),
             vmem(XE, YE, Z),
             vmem(3, 3, XE, YE, Z),
@@ -474,36 +512,43 @@
             vmem(R, 8, Z),
             vmem(4, YE, Z),
             vmem(4, YE, Z),
-            vmem(5, XE, 4, Z),
-            vmem(5, XE, 4, Z),
-            vmem(5, XE, 4, Z),
-            vmem(5, XE, 4, Z),
+            vmem(4, X + 2, 2, Z),
+            vmem(4, X + 2, 2, Z),
+            vmem(4, X + 2, 2, Z),
+            vmem(4, X + 2, 2, Z),
             vmem(4, XE, 4, Z),
             vmem(4, XE, 4, Z),
             vmem(4, XE, 4, Z),
             vmem(4, XE, 4, Z),
-            vmem(5, 4, YE, Z),
-            vmem(5, 4, YE, Z),
+            vmem(4, 2, YE, Z),
+            vmem(4, 2, YE, Z),
             vmem(4, 4, YE, Z),
             vmem(4, 4, YE, Z),
+            vmem(XE, YE, Z),
+            vmem(X, 4, Z),
+            vmem(X, 4, Z),
+            vmem(X, 4, Z),
+            vmem(X, 4, Z),
+            vmem(4, YE, Z),
+            vmem(4, YE, Z),
             vmem(8, 9, Z),
             vmem(8, 9, Z),
-            pltpu.SemaphoreType.DMA((20,)),
-            pltpu.SemaphoreType.DMA((20,)),
+            pltpu.SemaphoreType.DMA((24,)),
+            pltpu.SemaphoreType.DMA((24,)),
         ],
         compiler_params=pltpu.CompilerParams(
             collective_id=0, has_side_effects=True, vmem_limit_bytes=60 * 1024 * 1024
         ),
         name="steps",
     )(
-        particles.reshape(22, R, Y, Z),
-        masses.reshape(R, Y, Z),
-        occupied.reshape(R, Y, Z),
-        node_flags,
-        rowq,
-        kidx,
+        particles.transpose(0, 1, 3, 2, 4).reshape(22, S, Y * X, Z),
+        masses.transpose(0, 2, 1, 3).reshape(S, Y * X, Z),
+        occupied.transpose(0, 2, 1, 3).reshape(S, Y * X, Z),
+        node_flags.transpose(1, 0, 2).reshape(Y * X, Z),
+        depart.reshape(8, Z),
     )
-    return final_state.reshape(9, S, X, Y, Z), arrivals.reshape(9, 1, 1, 1, 8 * Z)
+    final_state = final_state.reshape(9, S, Y, X, Z).transpose(0, 1, 3, 2, 4)
+    return final_state, arrivals.reshape(9, 1, 1, 1, 8 * Z)
 
 
 def solution(mesh):

time: 73.2 us -> 55.8 us (0.76)
  local copies, waits for them, and re-layouts: 11.9 us -> 3.52 us
  Pallas kernels: 58.9 us -> 51.4 us
  other arithmetic: 1.3 us -> 0 us
    unnamed x6 -> x2, local copies, waits for them, and re-layouts: 11.9 us -> 3.52 us
    pallas_call x1, Pallas kernels: 58.9 us -> 51.4 us  [body(): pl.pallas_call(functools.partial(kernel, S, X, Y, n_gx, n_gy), out_shape=...]
    select_n x1 -> x0, other arithmetic: 1.3 us -> none  [body(): kidx = leaving % Z]
where the time goes in v1:
time: 55.8 us; the launch traced here: 55.6 us
  Pallas kernels  51.4 us (92%)
  local copies, waits for them, and re-layouts  3.52 us (6%)
  between operations  0.64 us (1%)
    pallas_call x1, Pallas kernels, body(): pl.pallas_call(functools.partial(kernel, S, X, Y, n_gx, n_gy), out_shape=...  51.4 us
    unnamed x2, local copies, waits for them, and re-layouts  3.52 us

profile of v1, /device:TPU:0, one launch (start us, length us, event | category | flops | bytes accessed | tf_op | source)
XLA Modules:
  0.0 55.6 jit_solution(12179574979296374928)
XLA Ops:
  0.6 51.4 %steps.1 = (f32[9,8,24,128]{3,2,1,0:T(8,128)}, f32[9,8,128]{2,1,0:T(8,128)}) custom-call(f32[22,8,24,128]{3,2,1,0:T(8,128)} %bitcast.17, f32[8,24,128]{2,1,0:T(8,128)} %bitcast.19, s32[8,24,128]{2,1,0:T(8,128)} %bitcast.20, s32[24,128]{1,0:T(8,128)} %bitcast.22, s32[8,128]{1,0:T(8,128)} %bitcast.23), custom_call_target="tpu_custom_call" | custom-call | tf_op jit(solution)/shard_map/steps/pallas_call | solution.py:493
  52.1 2.1 %copy.11 = f32[9,8,4,6,128]{4,2,3,1,0:T(4,128)} copy(f32[9,8,4,6,128]{4,2,3,1,0:T(4,128)} %bitcast.18) | data formatting | bytes 1769472
  54.2 1.4 %copy.12 = f32[9,1,1,1,1024]{4,3,2,1,0:T(1,128)} copy(f32[9,1,1,1,1024]{4,3,2,1,0:T(1,128)} %bitcast.21) | data formatting | bytes 73728

commit v2 on v1

--- a/solution.py
+++ b/solution.py
@@ -57,7 +57,7 @@
     out, arr,
     ST, PT, D, GZ, N0, N1, FL, VZ, VS, VALS, DM,
     PK, PKR, SYH0, SYL0, RYL0, RYH0, SYH1, SYL1, RYL1, RYH1,
-    RXL0, RXH0, RXL1, RXH1, NF, SFH, SFL, RFYL, RFYH, RFXL, RFXH, RES, ARR,
+    RXL0, RXH0, RXL1, RXH1, RC0, RC1, FB, RF, RES, ARR,
     send_sem, recv_sem,
 ):
     XE, YE = X + 4, Y + 4
@@ -147,8 +147,6 @@
         lax.fori_loop(0, R, body, 0)
 
     def deposit(nb, pairs):
-        D[...] = jnp.zeros(D.shape, F32)
-
         def body(p, carry):
             f = p // (3 * X)
             t = p - 3 * X
@@ -230,23 +228,44 @@
     def unpack(value, l):
         return value if l == 0 else pltpu.roll(value, Z - l, 1)
 
-    def velocities(step, N, SYH, SYL, RYL, RYH, RXL, RXH):
+    ident = depart[...].astype(F32)
+    line = jnp.floor((ident + 0.5) * (1.0 / Z))
+    kidx = ident - line * Z
+    slot = jnp.floor((line + 0.5) * (1.0 / (X * Y)))
+    cell = line - slot * (X * Y)
+    cell_x = jnp.floor((cell + 0.5) * (1.0 / Y))
+    rowq = (cell_x * S + slot) * 8.0 + (cell - cell_x * Y)
+
+    def direction_map():
+        rows = lax.broadcasted_iota(jnp.int32, (R * 8, Z), 0).astype(F32)
+        ks = lax.broadcasted_iota(jnp.int32, (Z, Z), 0).astype(F32)
+        total = jnp.zeros((R * 8, Z), F32)
+        for d in range(8):
+            here = jnp.where(rows == rowq[d : d + 1, :], d + 1.0, 0.0).astype(jnp.bfloat16)
+            hot = jnp.where(ks == kidx[d : d + 1, :], 1.0, 0.0).astype(jnp.bfloat16)
+            total = total + lax.dot_general(
+                here, hot, (((1,), (1,)), ((), ())), preferred_element_type=F32
+            )
+        DM[...] = total.reshape(R, 8, Z)
+
+    def velocities(step, N, SYH, SYL, RYL, RYH, RXL, RXH, RC):
         h = 1 + step
         lo = 2 - h
         xs = range(lo, X + 2 + h)
         nb = 3 if step == 0 else 4
-        base = 6 * step
+        base = 10 * step
         flag_copies = []
         if step == 0:
-            NF[...] = jnp.zeros(NF.shape, F32)
             for x in range(X):
                 fl = flags[pl.ds(x, Y, stride=X), :].astype(F32)
-                NF[x + 2, 2 : 2 + Y] = fl
-                SFH[x] = jnp.concatenate([fl[Y - 2 : Y], jnp.zeros((2, Z), F32)], axis=0)
-                SFL[x] = jnp.concatenate([jnp.zeros((2, Z), F32), fl[0:2]], axis=0)
+                FB[x] = fl
+                FL[x + 2, 2 : 2 + Y] = fl
             pl.semaphore_wait(barrier, 9)
-            flag_copies = [send(SFH, RFYL, 20, at(0, 1)), send(SFL, RFYH, 21, at(0, -1))]
         copy = send(PK.at[2 * step], PKR.at[2 * step], base, sibling)
+        if step == 0:
+            for d in range(8):
+                flag_copies.append(send(FB, RF.at[d], 28 + d, at(SHIFT_X[d], SHIFT_Y[d])))
+            direction_map()
         copy.wait()
         got = PKR[2 * step]
         got = jnp.where(is_low, pltpu.roll(got, Z - 1, 1), got)
@@ -257,41 +276,45 @@
                 N[n, x] = v
                 SYH[n, x - lo] = v[Y + lo : Y + lo + 2 * h]
                 SYL[n, x - lo] = v[lo : lo + 2 * h]
-        up = send(SYH, RYL, base + 1, at(0, 1))
-        down = send(SYL, RYH, base + 2, at(0, -1))
-        for copy in flag_copies:
-            copy.wait()
-        flag_copies = []
+        w = 2 * h
+        copies = [
+            send(N.at[:, X + lo : X + lo + w], RXL, base + 1, at(1, 0)),
+            send(N.at[:, lo : lo + w], RXH, base + 2, at(-1, 0)),
+            send(SYH, RYL, base + 3, at(0, 1)),
+            send(SYL, RYH, base + 4, at(0, -1)),
+            send(SYH.at[:, X : X + w], RC.at[0], base + 5, at(1, 1)),
+            send(SYH.at[:, 0:w], RC.at[1], base + 6, at(-1, 1)),
+            send(SYL.at[:, X : X + w], RC.at[2], base + 7, at(1, -1)),
+            send(SYL.at[:, 0:w], RC.at[3], base + 8, at(-1, -1)),
+        ]
         if step == 0:
-            for x in range(X):
-                NF[x + 2, 0:4] = NF[x + 2, 0:4] + RFYL[x]
-                NF[x + 2, Y : Y + 4] = NF[x + 2, Y : Y + 4] + RFYH[x]
-            flag_copies = [
-                send(NF.at[X : X + 4], RFXL, 22, at(1, 0)),
-                send(NF.at[0:4], RFXH, 23, at(-1, 0)),
-            ]
-        up.wait()
-        down.wait()
-        for n in range(4):
-            for x in xs:
-                N[n, x, lo : lo + 2 * h] = N[n, x, lo : lo + 2 * h] + RYL[n, x - lo]
-                N[n, x, Y + lo : Y + lo + 2 * h] = (
-                    N[n, x, Y + lo : Y + lo + 2 * h] + RYH[n, x - lo]
-                )
-        up = send(N.at[:, X + lo : X + lo + 2 * h], RXL, base + 3, at(1, 0))
-        down = send(N.at[:, lo : lo + 2 * h], RXH, base + 4, at(-1, 0))
+            VALS[...] = jnp.zeros(VALS.shape, F32)
+            D[...] = jnp.zeros(D.shape, F32)
+            VS[3] = jnp.zeros(VS.shape[1:], F32)
         for copy in flag_copies:
             copy.wait()
         if step == 0:
-            for x in range(XE):
-                v = NF[x]
-                if x < 4:
-                    v = v + RFXL[x]
-                if x >= X:
-                    v = v + RFXH[x - X]
-                FL[x] = v
-        up.wait()
-        down.wait()
+            ends_x = {-1: (X - 2, 0, 2), 0: (0, 2, X), 1: (0, X + 2, 2)}
+            ends_y = {-1: (Y - 2, 0, 2), 0: (0, 2, Y), 1: (0, Y + 2, 2)}
+            for d in range(8):
+                from_x, to_x, n_x = ends_x[-SHIFT_X[d]]
+                from_y, to_y, n_y = ends_y[-SHIFT_Y[d]]
+                for x in range(n_x):
+                    FL[to_x + x, to_y : to_y + n_y] = RF[d, from_x + x, from_y : from_y + n_y]
+        for copy in copies:
+            copy.wait()
+        for n in range(4):
+            for x in xs:
+                low = RYL[n, x - lo]
+                high = RYH[n, x - lo]
+                if x < lo + w:
+                    low = low + RC[0, n, x - lo]
+                    high = high + RC[2, n, x - lo]
+                if x >= X + lo:
+                    low = low + RC[1, n, x - X - lo]
+                    high = high + RC[3, n, x - X - lo]
+                N[n, x, lo : lo + w] = N[n, x, lo : lo + w] + low
+                N[n, x, Y + lo : Y + lo + w] = N[n, x, Y + lo : Y + lo + w] + high
         pack = jnp.zeros((YE, Z), F32)
         for x in xs:
             tot = []
@@ -314,14 +337,12 @@
                 moved = edge if l == 0 else pltpu.roll(edge, l, 1)
                 pack = jnp.where(lane == l, moved, pack)
         PK[2 * step + 1] = pack
-        copy = send(PK.at[2 * step + 1], PKR.at[2 * step + 1], base + 5, sibling)
+        copy = send(PK.at[2 * step + 1], PKR.at[2 * step + 1], base + 9, sibling)
         copy.wait()
         got = PKR[2 * step + 1]
         got = jnp.where(is_low, pltpu.roll(got, Z - 1, 1), got)
         got_high = jnp.where(is_low, got, 0.0)
         got_low = jnp.where(is_low, 0.0, got)
-        if step == 0:
-            VS[...] = jnp.zeros(VS.shape, F32)
         for k in range(3):
             for x in xs:
                 l = k * XE + x
@@ -373,9 +394,9 @@
                         t = wy[b] * (low + mid + high)
                         u[k] = plus(u[k], t)
                         if b == 0:
-                            uy[k] = -t
+                            uy[k] = t
                         elif b == 2:
-                            uy[k] = uy[k] + t
+                            uy[k] = t - uy[k]
                         elif b == 3:
                             uy[k] = uy[k] + far_y * t
                         uz[k] = plus(uz[k], wy[b] * (high - low))
@@ -384,9 +405,9 @@
                     t = wx * u[k]
                     speed[k] = plus(speed[k], t)
                     if a == 0:
-                        mx[k] = -t
+                        mx[k] = t
                     elif a == 2:
-                        mx[k] = mx[k] + t
+                        mx[k] = t - mx[k]
                     elif a == 3:
                         mx[k] = mx[k] + (4 * side - 2).astype(F32) * t
                     my[k] = plus(my[k], wx * uy[k])
@@ -421,26 +442,6 @@
             lax.fori_loop(0, 2 * S, edge_body, 0)
             lax.fori_loop(S, R - S, functools.partial(body, 3), 0)
 
-    ident = depart[...].astype(F32)
-    line = jnp.floor((ident + 0.5) * (1.0 / Z))
-    kidx = ident - line * Z
-    slot = jnp.floor((line + 0.5) * (1.0 / (X * Y)))
-    cell = line - slot * (X * Y)
-    cell_x = jnp.floor((cell + 0.5) * (1.0 / Y))
-    rowq = (cell_x * S + slot) * 8.0 + (cell - cell_x * Y)
-
-    def direction_map():
-        rows = lax.broadcasted_iota(jnp.int32, (R * 8, Z), 0).astype(F32)
-        ks = lax.broadcasted_iota(jnp.int32, (Z, Z), 0).astype(F32)
-        total = jnp.zeros((R * 8, Z), F32)
-        for d in range(8):
-            here = jnp.where(rows == rowq[d : d + 1, :], d + 1.0, 0.0).astype(jnp.bfloat16)
-            hot = jnp.where(ks == kidx[d : d + 1, :], 1.0, 0.0).astype(jnp.bfloat16)
-            total = total + lax.dot_general(
-                here, hot, (((1,), (1,)), ((), ())), preferred_element_type=F32
-            )
-        DM[...] = total.reshape(R, 8, Z)
-
     def extract():
         ks = lax.broadcasted_iota(jnp.int32, (Z, Z), 0).astype(F32)
         copies = []
@@ -464,24 +465,23 @@
                     )
             for d in ds:
                 copies.append(
-                    send(RES.at[d], ARR.at[d], 12 + d, at(SHIFT_X[d], SHIFT_Y[d]))
+                    send(RES.at[d], ARR.at[d], 20 + d, at(SHIFT_X[d], SHIFT_Y[d]))
                 )
         for copy in copies:
             copy.wait()
         for d in range(8):
             arr[:, d] = ARR[d]
 
+    D[...] = jnp.zeros(D.shape, F32)
     prepare(0)
     deposit(3, 3 * X)
     combine(0, 3, N0)
-    velocities(0, N0, SYH0, SYL0, RYL0, RYH0, RXL0, RXH0)
-    direction_map()
-    VALS[...] = jnp.zeros(VALS.shape, F32)
+    velocities(0, N0, SYH0, SYL0, RYL0, RYH0, RXL0, RXH0, RC0)
     gather(0)
     prepare(1)
     deposit(4, 3 * X + 2)
     combine(1, 4, N1)
-    velocities(1, N1, SYH1, SYL1, RYL1, RYH1, RXL1, RXH1)
+    velocities(1, N1, SYH1, SYL1, RYL1, RYH1, RXL1, RXH1, RC1)
     gather(1)
     extract()
 
@@ -524,17 +524,14 @@
             vmem(4, 2, YE, Z),
             vmem(4, 4, YE, Z),
             vmem(4, 4, YE, Z),
-            vmem(XE, YE, Z),
-            vmem(X, 4, Z),
-            vmem(X, 4, Z),
-            vmem(X, 4, Z),
-            vmem(X, 4, Z),
-            vmem(4, YE, Z),
-            vmem(4, YE, Z),
+            vmem(4, 4, 2, 2, Z),
+            vmem(4, 4, 4, 4, Z),
+            vmem(X, Y, Z),
+            vmem(8, X, Y, Z),
             vmem(8, 9, Z),
             vmem(8, 9, Z),
-            pltpu.SemaphoreType.DMA((24,)),
-            pltpu.SemaphoreType.DMA((24,)),
+            pltpu.SemaphoreType.DMA((36,)),
+            pltpu.SemaphoreType.DMA((36,)),
         ],
         compiler_params=pltpu.CompilerParams(
             collective_id=0, has_side_effects=True, vmem_limit_bytes=60 * 1024 * 1024

time: 55.8 us -> 51.4 us (0.921)
  Pallas kernels: 51.4 us -> 47 us
    pallas_call x1, Pallas kernels: 51.4 us -> 47 us  [body(): pl.pallas_call(functools.partial(kernel, S, X, Y, n_gx, n_gy), out_shape=...]
where the time goes in v2:
time: 51.4 us; the launch traced here: 51.1 us
  Pallas kernels  47 us (91%)
  local copies, waits for them, and re-layouts  3.52 us (7%)
  between operations  0.64 us (1%)
    pallas_call x1, Pallas kernels, body(): pl.pallas_call(functools.partial(kernel, S, X, Y, n_gx, n_gy), out_shape=...  47 us
    unnamed x2, local copies, waits for them, and re-layouts  3.52 us

profile of v2, /device:TPU:0, one launch (start us, length us, event | category | flops | bytes accessed | tf_op | source)
XLA Modules:
  0.0 51.1 jit_solution(11928110824344811647)
XLA Ops:
  0.6 47.0 %steps.1 = (f32[9,8,24,128]{3,2,1,0:T(8,128)}, f32[9,8,128]{2,1,0:T(8,128)}) custom-call(f32[22,8,24,128]{3,2,1,0:T(8,128)} %bitcast.17, f32[8,24,128]{2,1,0:T(8,128)} %bitcast.19, s32[8,24,128]{2,1,0:T(8,128)} %bitcast.20, s32[24,128]{1,0:T(8,128)} %bitcast.22, s32[8,128]{1,0:T(8,128)} %bitcast.23), custom_call_target="tpu_custom_call" | custom-call | tf_op jit(solution)/shard_map/steps/pallas_call | solution.py:493
  47.6 2.1 %copy.11 = f32[9,8,4,6,128]{4,2,3,1,0:T(4,128)} copy(f32[9,8,4,6,128]{4,2,3,1,0:T(4,128)} %bitcast.18) | data formatting | bytes 1769472
  49.7 1.4 %copy.12 = f32[9,1,1,1,1024]{4,3,2,1,0:T(1,128)} copy(f32[9,1,1,1,1024]{4,3,2,1,0:T(1,128)} %bitcast.21) | data formatting | bytes 73728
